TPU v7x, 32 devices: a whole 2x2x4 slice. The times are simulated.
32 devices in a mesh: row: 4 (over x, core), col: 8 (over z, y).
Axes of the slice: x: 2, y: 2, z: 4, core: 2. Of those that a mesh axis runs over, the one named last changes fastest.
Arguments:
- markov: bfloat16 [2, 256, 128, 128], P(None, 'col'), may hold values from -6 to 6
- omega: bfloat16 [32768, 64], P('col'), may hold values from -0.03125 to 0.03125
Outputs:
- denoised: float32 [2, 256, 128, 128], P(None, 'col')
All inputs are finite; a program needn't handle non-finite values.
Results may differ from a plain program's by a relative error of at most 0.0007.
Values may be sent and summed in bfloat16 or wider, within the bound.
No kernel may reach another device: no remote copies, remote signals or barrier semaphores. Data moves between devices by JAX's collectives and lax.ppermute only.
A program may use at most 64 MiB of HBM per device.

v0:
```python
import jax
import jax.numpy as jnp
from jax import lax
from jax.sharding import PartitionSpec as P

NS_STEPS = 8
norm_floor = 1e-06
highest = lax.Precision.HIGHEST


def shifted(block, axis, distance):
    devices = range(lax.axis_size(axis))
    route = [((i - distance) % len(devices), i) for i in devices]
    return lax.ppermute(block, axis, route)


def column_gram(matrix):
    return lax.dot_general(
        matrix,
        matrix,
        (((0,), (0,)), ((), ())),
        precision=highest,
        preferred_element_type=jnp.float32,
    )


def square_mul(left, right):
    return jnp.dot(left, right, precision=highest, preferred_element_type=jnp.float32)


def total_gram(partial_value):
    return lax.psum(partial_value, "row")


def orthonormal(sketch):
    gram = total_gram(column_gram(sketch))
    scale = 1.0 / jnp.sqrt(jnp.trace(gram) + norm_floor)
    coeffs = jnp.eye(gram.shape[0], dtype=jnp.float32) * scale
    for sweep in range(NS_STEPS):
        inner = square_mul(square_mul(coeffs.T, gram), coeffs)
        coeffs = 1.5 * coeffs - 0.5 * square_mul(coeffs, inner)
    return square_mul(sketch, coeffs)


def pick_half(pair, half_id):
    return jnp.where(half_id == 0, pair[0], pair[1])


def lag_sums(basis_blocks, column_rows, column_count):
    row_count, out_rows, rank_extent = basis_blocks.shape
    input_columns = column_rows.shape[1] // column_count
    start_total = jnp.zeros((out_rows, row_count + column_count, input_columns), jnp.float32)

    def add_row(row_position, running):
        orthonormal_row_vector = lax.dynamic_index_in_dim(
            basis_blocks, row_position, 0, keepdims=False
        )
        product = jnp.dot(orthonormal_row_vector, column_rows, preferred_element_type=jnp.float32)
        product = product.reshape(out_rows, column_count, input_columns)
        current_sum = lax.dynamic_slice_in_dim(running, row_position, column_count, 1)
        return lax.dynamic_update_slice_in_dim(running, current_sum + product, row_position, 1)

    return lax.fori_loop(0, row_count, add_row, start_total)


def local(markov, omega):
    n_rows = lax.axis_size("row")
    n_cols = lax.axis_size("col")
    row_position = lax.axis_index("row")
    col_id = lax.axis_index("col")
    halves, blocks, out_rows, input_columns = markov.shape
    rank_extent = omega.shape[1]
    bit_count = (n_rows - 1).bit_length()
    held = markov
    for bit_pos in range(bit_count):
        moved = shifted(held, "col", -(1 << bit_pos))
        held = jnp.where(row_position // (1 << bit_pos) % 2 == 1, moved, held)
    following = shifted(held, "col", -1)
    first_block = row_position + col_id
    window = jnp.concatenate(
        [pick_half(held, first_block // n_cols), pick_half(following, (first_block + 1) // n_cols)],
        axis=0,
    )
    omega_blocks = omega.reshape(blocks, input_columns, rank_extent)

    def slab_at(column_id):
        return lax.dynamic_slice_in_dim(window, column_id, blocks, 0).reshape(
            blocks * out_rows, input_columns
        )

    def range_step(column_id, running):
        weights = lax.dynamic_index_in_dim(omega_blocks, column_id, 0, keepdims=False)
        return running + jnp.dot(slab_at(column_id), weights, preferred_element_type=jnp.float32)

    partial_value = lax.fori_loop(
        0, blocks, range_step, jnp.zeros((blocks * out_rows, rank_extent), jnp.float32)
    )
    sketch = lax.psum(partial_value, "col")
    basis = orthonormal(sketch).astype(jnp.bfloat16)

    def projection_update(column_id, running):
        term = lax.dot_general(
            basis, slab_at(column_id), (((0,), (0,)), ((), ())), preferred_element_type=jnp.float32
        )
        return lax.dynamic_update_slice_in_dim(running, term, column_id * input_columns, 1)

    projected_matrix = lax.fori_loop(
        0, blocks, projection_update, jnp.zeros((rank_extent, blocks * input_columns), jnp.float32)
    )
    projected_matrix = lax.psum(projected_matrix, "row").astype(jnp.bfloat16)
    basis_blocks = basis.reshape(blocks, out_rows, rank_extent)
    local_sums = lag_sums(basis_blocks, projected_matrix, blocks).transpose(1, 0, 2)
    for bit_pos in range(bit_count):
        moved = shifted(local_sums.astype(jnp.bfloat16), "col", 1 << bit_pos).astype(
            local_sums.dtype
        )
        local_sums = jnp.where(row_position // (1 << bit_pos) % 2 == 1, moved, local_sums)
    carried = shifted(local_sums[blocks:].astype(jnp.bfloat16), "col", 1).astype(jnp.float32)
    own_half = (col_id < row_position).astype(jnp.int32)
    prev_col = (col_id + n_cols - 1) % n_cols
    carry_half = (prev_col + n_cols * (prev_col < row_position).astype(jnp.int32) + 1) // n_cols
    owned = jnp.stack(
        [
            jnp.where(own_half == half_id, local_sums[:blocks], 0.0)
            + jnp.where(carry_half == half_id, carried, 0.0)
            for half_id in range(2)
        ]
    )
    totals = lax.psum(owned, "row")
    total_rows = blocks * n_rows
    total_cols = blocks * n_cols
    lag_ids = (
        jnp.arange(2, dtype=jnp.int32)[:, None] * total_cols
        + col_id * blocks
        + jnp.arange(blocks, dtype=jnp.int32)[None, :]
    )
    counts = jnp.maximum(
        jnp.minimum(lag_ids, total_rows - 1) - jnp.maximum(0, lag_ids - total_cols + 1) + 1, 0
    )
    counts_f = counts.astype(jnp.float32)[:, :, None, None]
    measured = markov.astype(jnp.float32)
    averaged = totals / jnp.maximum(counts_f, 1.0)
    return jnp.where(counts_f > 0, 0.5 * measured + 0.5 * averaged, measured)


def solution(mesh):
    in_specs = (P(None, "col", None, None), P("col", None))
    out_specs = P(None, "col", None, None)
    return jax.shard_map(local, mesh=mesh, in_specs=in_specs, out_specs=out_specs, check_vma=False)
```

profile of v0, /device:TPU:0, one launch (start us, length us, event | category | flops | bytes accessed | tf_op | source)
XLA Modules:
  0.0 767.1 jit_solution(6744331033921523730)
XLA Ops:
  6.5 6.0 collective-permute-start
  12.6 45.2 %collective-permute-done = bf16[2,32,128,128]{3,2,1,0:T(8,128)(2,1)} collective-permute-done((bf16[2,32,128,128]{3,2,1,0:T(8,128)(2,1)}, bf16[2,32,128,128]{3,2,1,0:T(8,128)(2,1)}, u32[]{:S(2)}, u32[]{:S(2)}) %collective-permute-start) | collective-permute-done | bytes 2097184 | tf_op jit(solution)/shard_map/ppermute | solution.py:14
  61.2 45.1 %collective-permute-done.1 = bf16[2,32,128,128]{3,2,1,0:T(8,128)(2,1)} collective-permute-done((bf16[2,32,128,128]{3,2,1,0:T(8,128)(2,1)S(1)}, bf16[2,32,128,128]{3,2,1,0:T(8,128)(2,1)}, u32[]{:S(2)}, u32[]{:S(2)}) %collective-permute-start.1) | collective-permute-done | bytes 2097184 | tf_op jit(solution)/shard_map/ppermute | solution.py:14
  107.8 7.0 collective-permute-start.2
  117.8 40.5 %collective-permute-done.2 = bf16[2,32,128,128]{3,2,1,0:T(8,128)(2,1)S(1)} collective-permute-done((bf16[2,32,128,128]{3,2,1,0:T(8,128)(2,1)}, bf16[2,32,128,128]{3,2,1,0:T(8,128)(2,1)S(1)}, u32[]{:S(2)}, u32[]{:S(2)}) %collective-permute-start.2) | collective-permute-done | bytes 2097184 | tf_op jit(solution)/shard_map/ppermute | solution.py:14
  158.6 92.9 %while.42 = (s32[]{:T(128)}, f32[4096,64]{0,1:T(8,128)}, bf16[64,128,128]{2,1,0:T(8,128)(2,1)S(1)}, bf16[32,128,64]{2,1,0:T(8,128)(2,1)}, s32[]{:T(128)}, /*index=5*/s32[]{:T(128)}) while((s32[]{:T(128)}, f32[4096,64]{0,1:T(8,128)}, bf16[64,128,128]{2,1,0:T(8,128)(2,1)S(1)}, bf16[32,128,64]{2,1,0:T(8,128)(2,1)}, s32[]{:T(128)}, ...), condition=%wide.region_1.2_spmd.clone, body=%wide.region_0.1_spmd.clone.sunk | while | flops 67633152 | bytes 5276243 | solution.py:95
  251.6 81.7 %all-reduce.4.cloned.1.call-done = f32[4096,64]{0,1:T(8,128)} async-done(((f32[4096,64]{0,1:T(8,128)}), f32[4096,64]{0,1:T(8,128)}) %all-reduce.4.cloned.1.call-update) | async-done | bytes 1048592 | tf_op jit(solution)/shard_map/psum | solution.py:98
  335.9 11.3 %psum.29 = f32[64,64]{1,0:T(8,128)S(1)} all-reduce(f32[64,64]{1,0:T(8,128)S(1)} %fusion.39), channel_id=1, replica_groups=mesh['row'=4,'col'=8] {'row'}, use_global_device_ids=true, to_apply=%region_3.4 | all-reduce | flops 4096 | bytes 32768 | tf_op jit(solution)/shard_map/psum | solution.py:32
  359.6 39.2 %while.40 = (s32[]{:T(128)}, f32[64,4096]{1,0:T(8,128)}, bf16[64,128,128]{2,1,0:T(8,128)(2,1)S(1)}, bf16[4096,64]{1,0:T(8,128)(2,1)S(1)}, s32[]{:T(128)}, /*index=5*/s32[]{:T(128)}, s32[]{:T(128)}, s32[]{:T(128)}) while((s32[]{:T(128)}, f32[64,4096]{1,0:T(8,128)}, bf16[64,128,128]{2,1,0:T(8,128)(2,1)S(1)}, bf16[4096,64]{1,0:T(8,128)(2,1)S(1)}, ...), condition=%wide.region_6.7_spmd, body=%wide.region_5.6_spmd.sunk | while | flops 67108872 | bytes 3702923 | solution.py:107
  398.9 26.3 %all-reduce.7 = bf16[64,4096]{1,0:T(8,128)(2,1)S(1)} all-reduce(f32[64,4096]{1,0:T(8,128)} %get-tuple-element.243), channel_id=1, replica_groups=mesh['row'=4,'col'=8] {'row'}, use_global_device_ids=true, to_apply=%region_7.8 | all-reduce | flops 262144 | bytes 1572864 | tf_op jit(solution)/shard_map/psum | solution.py:110
  427.7 108.3 %while.41 = (s32[]{:T(128)}, f32[128,64,128]{2,0,1:T(8,128)}, bf16[32,128,64]{1,2,0:T(8,128)(2,1)}, bf16[64,4096]{1,0:T(8,128)(2,1)S(1)}, s32[]{:T(128)}) while((s32[]{:T(128)}, f32[128,64,128]{2,0,1:T(8,128)}, bf16[32,128,64]{1,2,0:T(8,128)(2,1)}, bf16[64,4096]{1,0:T(8,128)(2,1)S(1)}, s32[]{:T(128)}) %tuple.87), condition=%wide.region_9.10_spmd, body=%wide.region_8.9_spmd.sunk | while | flops 67633152 | bytes 4736061 | solution.py:63
  427.7 3.4 add_dynamic-update-slice_fusion.2
  431.1 3.4 add_dynamic-update-slice_fusion.2
  434.5 3.4 add_dynamic-update-slice_fusion.2
  437.9 3.4 add_dynamic-update-slice_fusion.2
  441.3 3.4 add_dynamic-update-slice_fusion.2
  444.7 3.4 add_dynamic-update-slice_fusion.2
  448.0 3.4 add_dynamic-update-slice_fusion.2
  451.4 3.4 add_dynamic-update-slice_fusion.2
  454.8 3.4 add_dynamic-update-slice_fusion.2
  458.2 3.4 add_dynamic-update-slice_fusion.2
  461.6 3.4 add_dynamic-update-slice_fusion.2
  465.0 3.4 add_dynamic-update-slice_fusion.2
  468.4 3.4 add_dynamic-update-slice_fusion.2
  471.7 3.4 add_dynamic-update-slice_fusion.2
  475.1 3.4 add_dynamic-update-slice_fusion.2
  478.5 3.4 add_dynamic-update-slice_fusion.2
  481.9 3.4 add_dynamic-update-slice_fusion.2
  485.3 3.4 add_dynamic-update-slice_fusion.2
  488.7 3.4 add_dynamic-update-slice_fusion.2
  492.1 3.4 add_dynamic-update-slice_fusion.2
  495.4 3.4 add_dynamic-update-slice_fusion.2
  498.8 3.4 add_dynamic-update-slice_fusion.2
  502.2 3.4 add_dynamic-update-slice_fusion.2
  505.6 3.4 add_dynamic-update-slice_fusion.2
  509.0 3.4 add_dynamic-update-slice_fusion.2
  512.4 3.4 add_dynamic-update-slice_fusion.2
  515.8 3.4 add_dynamic-update-slice_fusion.2
  519.1 3.4 add_dynamic-update-slice_fusion.2
  522.5 3.4 add_dynamic-update-slice_fusion.2
  525.9 3.4 add_dynamic-update-slice_fusion.2
  529.3 3.4 add_dynamic-update-slice_fusion.2
  532.7 3.4 add_dynamic-update-slice_fusion.2
  539.3 50.2 %collective-permute-done.3 = bf16[64,128,128]{2,1,0:T(8,128)(2,1)S(1)} collective-permute-done((bf16[64,128,128]{2,1,0:T(8,128)(2,1)S(1)}, bf16[64,128,128]{2,1,0:T(8,128)(2,1)S(1)}, u32[]{:S(2)}, u32[]{:S(2)}) %collective-permute-start.3) | collective-permute-done | bytes 2097184 | tf_op jit(solution)/shard_map/ppermute | solution.py:14
  590.2 48.9 %collective-permute-done.4 = bf16[64,128,128]{2,1,0:T(8,128)(2,1)S(1)} collective-permute-done((bf16[64,128,128]{2,1,0:T(8,128)(2,1)S(1)}, bf16[64,128,128]{2,1,0:T(8,128)(2,1)S(1)}, u32[]{:S(2)}, u32[]{:S(2)}) %collective-permute-start.4) | collective-permute-done | bytes 2097184 | tf_op jit(solution)/shard_map/ppermute | solution.py:14
  642.6 26.4 %collective-permute-done.5 = bf16[32,128,128]{2,1,0:T(8,128)(2,1)S(1)} collective-permute-done((bf16[32,128,128]{2,1,0:T(8,128)(2,1)S(1)}, bf16[32,128,128]{2,1,0:T(8,128)(2,1)S(1)}, u32[]{:S(2)}, u32[]{:S(2)}) %collective-permute-start.5) | collective-permute-done | bytes 1048608 | tf_op jit(solution)/shard_map/ppermute | solution.py:14
  673.6 81.6 %all-reduce.6.cloned.1.call-done = f32[2,32,128,128]{3,2,1,0:T(8,128)} async-done(((f32[2,32,128,128]{3,2,1,0:T(8,128)}), f32[2,32,128,128]{3,2,1,0:T(8,128)}) %all-reduce.6.cloned.1.call-update) | async-done | bytes 4194320 | tf_op jit(solution)/shard_map/psum | solution.py:129
  755.3 5.0 convert_select_fusion
  (193 shorter events, 168.3 us)
Async XLA Ops:
  6.5 326.8 %all-reduce.4.cloned.1.call-start = ((), (), s32[]{:S(2)}) async-start(), calls=%async_computation | async-start | bytes 2097152 | tf_op jit(solution)/shard_map/psum | solution.py:98
  6.5 51.2 %collective-permute-start = (bf16[2,32,128,128]{3,2,1,0:T(8,128)(2,1)}, bf16[2,32,128,128]{3,2,1,0:T(8,128)(2,1)}, u32[]{:S(2)}, u32[]{:S(2)}) collective-permute-start(bf16[2,32,128,128]{3,2,1,0:T(8,128)(2,1)} %param.8), channel_id=1, source_target_pairs={{1,0},{2,1},{3,2},{4,3},{5,4},{6,5},{7,6},{0,7},{9,8},{10,9},{11,1... | collective-permute-start | bytes 6291464 | tf_op jit(solution)/shard_map/ppermute | solution.py:14
  59.6 46.7 %collective-permute-start.1 = (bf16[2,32,128,128]{3,2,1,0:T(8,128)(2,1)S(1)}, bf16[2,32,128,128]{3,2,1,0:T(8,128)(2,1)}, u32[]{:S(2)}, u32[]{:S(2)}) collective-permute-start(bf16[2,32,128,128]{3,2,1,0:T(8,128)(2,1)S(1)} %broadcast_select_fusion), channel_id=1, source_target_pairs={{2,0},{3,1},{4,2},{5,3},{6,4},{7,5},{0,6},{1,7},{10,8},{11,9},{12,... | collective-permute-start | bytes 6291464 | tf_op jit(solution)/shard_map/ppermute | solution.py:14
  61.2 53.6 %copy-start.4 = (bf16[4096,64]{0,1:T(8,128)(2,1)S(1)}, bf16[4096,64]{0,1:T(8,128)(2,1)}, u32[]{:S(2)}) copy-start(bf16[4096,64]{0,1:T(8,128)(2,1)} %param.9) | copy-start | bytes 1572868
  107.8 50.5 %collective-permute-start.2 = (bf16[2,32,128,128]{3,2,1,0:T(8,128)(2,1)}, bf16[2,32,128,128]{3,2,1,0:T(8,128)(2,1)S(1)}, u32[]{:S(2)}, u32[]{:S(2)}) collective-permute-start(bf16[2,32,128,128]{3,2,1,0:T(8,128)(2,1)} %broadcast_select_fusion.1), channel_id=1, source_target_pairs={{1,0},{2,1},{3,2},{4,3},{5,4},{6,5},{7,6},{0,7},{9,8},{10,9},{11,1... | collective-permute-start | bytes 6291464 | tf_op jit(solution)/shard_map/ppermute | solution.py:14
  251.5 503.7 %all-reduce.6.cloned.1.call-start = ((), (), s32[]{:S(2)}) async-start(), calls=%async_computation.1 | async-start | bytes 8388608 | tf_op jit(solution)/shard_map/psum | solution.py:129
  333.3 19.9 %copy-start.2 = (f32[4096,64]{0,1:T(8,128)S(1)}, f32[4096,64]{0,1:T(8,128)}, u32[]{:S(2)}) copy-start(f32[4096,64]{0,1:T(8,128)} %all-reduce.4.cloned.1.call-done) | copy-start | bytes 3145732
  536.1 53.4 %copy-start = (f32[128,64,128]{2,0,1:T(8,128)S(1)}, f32[128,64,128]{2,0,1:T(8,128)}, u32[]{:S(2)}) copy-start(f32[128,64,128]{2,0,1:T(8,128)} %get-tuple-element.244) | copy-start | bytes 12582916
  538.8 50.7 %collective-permute-start.3 = (bf16[64,128,128]{2,1,0:T(8,128)(2,1)S(1)}, bf16[64,128,128]{2,1,0:T(8,128)(2,1)S(1)}, u32[]{:S(2)}, u32[]{:S(2)}) collective-permute-start(bf16[64,128,128]{2,1,0:T(8,128)(2,1)S(1)} %bitcast_convert_fusion), channel_id=1, source_target_pairs={{7,0},{0,1},{1,2},{2,3},{3,4},{4,5},{5,6},{6,7},{15,8},{8,9},{9,10... | collective-permute-start | bytes 6291464 | tf_op jit(solution)/shard_map/ppermute | solution.py:14
  590.1 48.9 %collective-permute-start.4 = (bf16[64,128,128]{2,1,0:T(8,128)(2,1)S(1)}, bf16[64,128,128]{2,1,0:T(8,128)(2,1)S(1)}, u32[]{:S(2)}, u32[]{:S(2)}) collective-permute-start(bf16[64,128,128]{2,1,0:T(8,128)(2,1)S(1)} %fusion.10), channel_id=1, source_target_pairs={{6,0},{7,1},{0,2},{1,3},{2,4},{3,5},{4,6},{5,7},{14,8},{15,9},{8,1... | collective-permute-start | bytes 6291464 | tf_op jit(solution)/shard_map/ppermute | solution.py:14
  640.3 2.0 copy-start.1
  642.4 26.5 %collective-permute-start.5 = (bf16[32,128,128]{2,1,0:T(8,128)(2,1)S(1)}, bf16[32,128,128]{2,1,0:T(8,128)(2,1)S(1)}, u32[]{:S(2)}, u32[]{:S(2)}) collective-permute-start(bf16[32,128,128]{2,1,0:T(8,128)(2,1)S(1)} %slice.43), channel_id=1, source_target_pairs={{7,0},{0,1},{1,2},{2,3},{3,4},{4,5},{5,6},{6,7},{15,8},{8,9},{9,10... | collective-permute-start | bytes 3145736 | tf_op jit(solution)/shard_map/ppermute | solution.py:14
  673.5 81.8 %copy-start.3 = (bf16[2,32,128,128]{3,2,1,0:T(8,128)(2,1)S(1)}, bf16[2,32,128,128]{3,2,1,0:T(8,128)(2,1)}, u32[]{:S(2)}) copy-start(bf16[2,32,128,128]{3,2,1,0:T(8,128)(2,1)} %param.8) | copy-start | bytes 6291460
Sparse Core Ops, SparseCore 0:
  251.7 81.5 all-reduce.3
  673.6 81.6 all-reduce.5
where the time goes:
time: 770 us; the launch traced here: 767 us
  waiting for transfers between devices  420 us (55%)
  matrix products  242 us (31%)
  blocking collectives  37.7 us (5%)
  other arithmetic  20.1 us (3%)
  local copies, waits for them, and re-layouts  17 us (2%)
  starting transfers between devices  15.3 us (2%)
  between operations  14.5 us (2%)
    ppermute x6, waiting for transfers between devices, shifted(): return lax.ppermute(block, axis, route)  256 us
    dot_general x32, matrix products, add_row(): jnp.dot(orthonormal_row_vector, column_rows, preferred_element_type=jnp.f...  108 us
    dot_general x32, matrix products, range_step(): jnp.dot(slab_at(column_id), weights, preferred_element_type=jnp.float32)  89.3 us
    psum x1, waiting for transfers between devices, local(): sketch = lax.psum(partial_value, 'col')  81.7 us
    psum x1, waiting for transfers between devices, local(): totals = lax.psum(owned, 'row')  81.6 us
    dot_general x32, matrix products, projection_update(): lax.dot_general(basis, slab_at(column_id), (((0,), (0,)), ((), ())), pref...  35.7 us
    psum x1, blocking collectives, local(): projected_matrix = lax.psum(projected_matrix, 'row').astype(jnp.bfloat16)  26.3 us
  transfers between devices with their start and end apart: 8, of which 8 were waited for; matrix products, arithmetic and copies ran while one was open for 0% of the time, Pallas kernels for 0%

commit v1 on v0

--- a/solution.py
+++ b/solution.py
@@ -95,7 +95,8 @@
     partial_value = lax.fori_loop(
         0, blocks, range_step, jnp.zeros((blocks * out_rows, rank_extent), jnp.float32)
     )
-    sketch = lax.psum(partial_value, "col")
+    answer = lax.all_gather(partial_value, "col")
+    sketch = jnp.sum(answer, 0)
     basis = orthonormal(sketch).astype(jnp.bfloat16)
 
     def projection_update(column_id, running):

time: 770 us -> 825 us (1.071)
  waiting for transfers between devices: 420 us -> 467 us
    all_gather x0 -> x1, waiting for transfers between devices: none -> 128 us  [local(): answer = lax.all_gather(partial_value, 'col')]
    psum x1 -> x0, waiting for transfers between devices: 81.7 us -> none  [local(): sketch = lax.psum(partial_value, 'col')]
where the time goes in v1:
time: 825 us; the launch traced here: 822 us
  waiting for transfers between devices  467 us (57%)
  matrix products  241 us (29%)
  blocking collectives  36.9 us (4%)
  local copies, waits for them, and re-layouts  25.1 us (3%)
  other arithmetic  22.2 us (3%)
  starting transfers between devices  15.4 us (2%)
  between operations  14.5 us (2%)
    ppermute x6, waiting for transfers between devices, shifted(): return lax.ppermute(block, axis, route)  256 us
    all_gather x1, waiting for transfers between devices, local(): answer = lax.all_gather(partial_value, 'col')  128 us
    dot_general x32, matrix products, add_row(): jnp.dot(orthonormal_row_vector, column_rows, preferred_element_type=jnp.f...  108 us
    dot_general x32, matrix products, range_step(): jnp.dot(slab_at(column_id), weights, preferred_element_type=jnp.float32)  89.2 us
    psum x1, waiting for transfers between devices, local(): totals = lax.psum(owned, 'row')  82.6 us
    dot_general x32, matrix products, projection_update(): lax.dot_general(basis, slab_at(column_id), (((0,), (0,)), ((), ())), pref...  35.7 us
    psum x1, blocking collectives, local(): projected_matrix = lax.psum(projected_matrix, 'row').astype(jnp.bfloat16)  26.4 us
  transfers between devices with their start and end apart: 8, of which 8 were waited for; matrix products, arithmetic and copies ran while one was open for 0% of the time, Pallas kernels for 0%

profile of v1, /device:TPU:0, one launch (start us, length us, event | category | flops | bytes accessed | tf_op | source)
XLA Modules:
  0.0 822.0 jit_solution(9660652616724607382)
XLA Ops:
  6.5 6.0 collective-permute-start
  12.6 45.2 %collective-permute-done = bf16[2,32,128,128]{3,2,1,0:T(8,128)(2,1)} collective-permute-done((bf16[2,32,128,128]{3,2,1,0:T(8,128)(2,1)}, bf16[2,32,128,128]{3,2,1,0:T(8,128)(2,1)}, u32[]{:S(2)}, u32[]{:S(2)}) %collective-permute-start) | collective-permute-done | bytes 2097184 | tf_op jit(solution)/shard_map/ppermute | solution.py:14
  61.2 45.1 %collective-permute-done.1 = bf16[2,32,128,128]{3,2,1,0:T(8,128)(2,1)} collective-permute-done((bf16[2,32,128,128]{3,2,1,0:T(8,128)(2,1)S(1)}, bf16[2,32,128,128]{3,2,1,0:T(8,128)(2,1)}, u32[]{:S(2)}, u32[]{:S(2)}) %collective-permute-start.1) | collective-permute-done | bytes 2097184 | tf_op jit(solution)/shard_map/ppermute | solution.py:14
  107.8 7.0 collective-permute-start.2
  117.8 40.5 %collective-permute-done.2 = bf16[2,32,128,128]{3,2,1,0:T(8,128)(2,1)S(1)} collective-permute-done((bf16[2,32,128,128]{3,2,1,0:T(8,128)(2,1)}, bf16[2,32,128,128]{3,2,1,0:T(8,128)(2,1)S(1)}, u32[]{:S(2)}, u32[]{:S(2)}) %collective-permute-start.2) | collective-permute-done | bytes 2097184 | tf_op jit(solution)/shard_map/ppermute | solution.py:14
  158.6 92.9 %while.42 = (s32[]{:T(128)}, f32[4096,64]{0,1:T(8,128)}, bf16[64,128,128]{2,1,0:T(8,128)(2,1)S(1)}, bf16[32,128,64]{2,1,0:T(8,128)(2,1)}, s32[]{:T(128)}, /*index=5*/s32[]{:T(128)}) while((s32[]{:T(128)}, f32[4096,64]{0,1:T(8,128)}, bf16[64,128,128]{2,1,0:T(8,128)(2,1)S(1)}, bf16[32,128,64]{2,1,0:T(8,128)(2,1)}, s32[]{:T(128)}, ...), condition=%wide.region_1.2_spmd.clone, body=%wide.region_0.1_spmd.clone.sunk | while | flops 67633152 | bytes 5276243 | solution.py:95
  251.5 127.9 %all-gather.3.cloned.1.call-done = f32[32768,64]{0,1:T(8,128)} async-done(((f32[4096,64]{0,1:T(8,128)}), f32[32768,64]{0,1:T(8,128)}) %all-gather.3.cloned.1.call-update) | async-done | bytes 8388624 | tf_op jit(solution)/shard_map/all_gather | solution.py:98
  379.4 8.1 copy.13
  390.6 10.4 %psum.21 = f32[64,64]{1,0:T(8,128)S(1)} all-reduce(f32[64,64]{1,0:T(8,128)S(1)} %fusion.39), channel_id=1, replica_groups=mesh['row'=4,'col'=8] {'row'}, use_global_device_ids=true, to_apply=%region_3.4 | all-reduce | flops 4096 | bytes 32768 | tf_op jit(solution)/shard_map/psum | solution.py:32
  413.5 39.2 %while.40 = (s32[]{:T(128)}, f32[64,4096]{1,0:T(8,128)}, bf16[64,128,128]{2,1,0:T(8,128)(2,1)S(1)}, bf16[4096,64]{1,0:T(8,128)(2,1)S(1)}, s32[]{:T(128)}, /*index=5*/s32[]{:T(128)}, s32[]{:T(128)}, s32[]{:T(128)}) while((s32[]{:T(128)}, f32[64,4096]{1,0:T(8,128)}, bf16[64,128,128]{2,1,0:T(8,128)(2,1)S(1)}, bf16[4096,64]{1,0:T(8,128)(2,1)S(1)}, ...), condition=%wide.region_6.7_spmd, body=%wide.region_5.6_spmd.sunk | while | flops 67108872 | bytes 3702923 | solution.py:108
  452.7 26.4 %all-reduce.4 = bf16[64,4096]{1,0:T(8,128)(2,1)S(1)} all-reduce(f32[64,4096]{1,0:T(8,128)} %get-tuple-element.243), channel_id=1, replica_groups=mesh['row'=4,'col'=8] {'row'}, use_global_device_ids=true, to_apply=%region_7.8 | all-reduce | flops 262144 | bytes 1572864 | tf_op jit(solution)/shard_map/psum | solution.py:111
  481.6 108.3 %while.41 = (s32[]{:T(128)}, f32[128,64,128]{2,0,1:T(8,128)}, bf16[32,128,64]{1,2,0:T(8,128)(2,1)}, bf16[64,4096]{1,0:T(8,128)(2,1)S(1)}, s32[]{:T(128)}) while((s32[]{:T(128)}, f32[128,64,128]{2,0,1:T(8,128)}, bf16[32,128,64]{1,2,0:T(8,128)(2,1)}, bf16[64,4096]{1,0:T(8,128)(2,1)S(1)}, s32[]{:T(128)}) %tuple.89), condition=%wide.region_9.10_spmd, body=%wide.region_8.9_spmd.sunk | while | flops 67633152 | bytes 4736061 | solution.py:63
  485.0 3.4 add_dynamic-update-slice_fusion.2
  488.4 3.4 add_dynamic-update-slice_fusion.2
  491.8 3.4 add_dynamic-update-slice_fusion.2
  495.2 3.4 add_dynamic-update-slice_fusion.2
  498.6 3.4 add_dynamic-update-slice_fusion.2
  502.0 3.4 add_dynamic-update-slice_fusion.2
  505.3 3.4 add_dynamic-update-slice_fusion.2
  508.7 3.4 add_dynamic-update-slice_fusion.2
  512.1 3.4 add_dynamic-update-slice_fusion.2
  515.5 3.4 add_dynamic-update-slice_fusion.2
  518.9 3.4 add_dynamic-update-slice_fusion.2
  522.3 3.4 add_dynamic-update-slice_fusion.2
  525.7 3.4 add_dynamic-update-slice_fusion.2
  529.0 3.4 add_dynamic-update-slice_fusion.2
  532.4 3.4 add_dynamic-update-slice_fusion.2
  535.8 3.4 add_dynamic-update-slice_fusion.2
  539.2 3.4 add_dynamic-update-slice_fusion.2
  542.6 3.4 add_dynamic-update-slice_fusion.2
  546.0 3.4 add_dynamic-update-slice_fusion.2
  549.3 3.4 add_dynamic-update-slice_fusion.2
  552.7 3.4 add_dynamic-update-slice_fusion.2
  556.1 3.4 add_dynamic-update-slice_fusion.2
  559.5 3.4 add_dynamic-update-slice_fusion.2
  562.9 3.4 add_dynamic-update-slice_fusion.2
  566.3 3.4 add_dynamic-update-slice_fusion.2
  569.7 3.4 add_dynamic-update-slice_fusion.2
  573.0 3.4 add_dynamic-update-slice_fusion.2
  576.4 3.4 add_dynamic-update-slice_fusion.2
  579.8 3.4 add_dynamic-update-slice_fusion.2
  583.2 3.4 add_dynamic-update-slice_fusion.2
  586.6 3.4 add_dynamic-update-slice_fusion.2
  593.3 50.1 %collective-permute-done.3 = bf16[64,128,128]{2,1,0:T(8,128)(2,1)S(1)} collective-permute-done((bf16[64,128,128]{2,1,0:T(8,128)(2,1)S(1)}, bf16[64,128,128]{2,1,0:T(8,128)(2,1)S(1)}, u32[]{:S(2)}, u32[]{:S(2)}) %collective-permute-start.3) | collective-permute-done | bytes 2097184 | tf_op jit(solution)/shard_map/ppermute | solution.py:14
  644.1 48.9 %collective-permute-done.4 = bf16[64,128,128]{2,1,0:T(8,128)(2,1)S(1)} collective-permute-done((bf16[64,128,128]{2,1,0:T(8,128)(2,1)S(1)}, bf16[64,128,128]{2,1,0:T(8,128)(2,1)S(1)}, u32[]{:S(2)}, u32[]{:S(2)}) %collective-permute-start.4) | collective-permute-done | bytes 2097184 | tf_op jit(solution)/shard_map/ppermute | solution.py:14
  696.5 26.4 %collective-permute-done.5 = bf16[32,128,128]{2,1,0:T(8,128)(2,1)S(1)} collective-permute-done((bf16[32,128,128]{2,1,0:T(8,128)(2,1)S(1)}, bf16[32,128,128]{2,1,0:T(8,128)(2,1)S(1)}, u32[]{:S(2)}, u32[]{:S(2)}) %collective-permute-start.5) | collective-permute-done | bytes 1048608 | tf_op jit(solution)/shard_map/ppermute | solution.py:14
  727.6 82.6 %all-reduce.3.cloned.1.call-done = f32[2,32,128,128]{3,2,1,0:T(8,128)} async-done(((f32[2,32,128,128]{3,2,1,0:T(8,128)}), f32[2,32,128,128]{3,2,1,0:T(8,128)}) %all-reduce.3.cloned.1.call-update) | async-done | bytes 4194320 | tf_op jit(solution)/shard_map/psum | solution.py:130
  810.1 5.0 convert_select_fusion
  (193 shorter events, 172.2 us)
Async XLA Ops:
  6.5 372.9 %all-gather.3.cloned.1.call-start = ((), (), s32[]{:S(2)}) async-start(), calls=%async_computation.1 | async-start | bytes 9437184 | tf_op jit(solution)/shard_map/all_gather | solution.py:98
  6.5 51.2 %collective-permute-start = (bf16[2,32,128,128]{3,2,1,0:T(8,128)(2,1)}, bf16[2,32,128,128]{3,2,1,0:T(8,128)(2,1)}, u32[]{:S(2)}, u32[]{:S(2)}) collective-permute-start(bf16[2,32,128,128]{3,2,1,0:T(8,128)(2,1)} %param.8), channel_id=1, source_target_pairs={{1,0},{2,1},{3,2},{4,3},{5,4},{6,5},{7,6},{0,7},{9,8},{10,9},{11,1... | collective-permute-start | bytes 6291464 | tf_op jit(solution)/shard_map/ppermute | solution.py:14
  59.6 46.7 %collective-permute-start.1 = (bf16[2,32,128,128]{3,2,1,0:T(8,128)(2,1)S(1)}, bf16[2,32,128,128]{3,2,1,0:T(8,128)(2,1)}, u32[]{:S(2)}, u32[]{:S(2)}) collective-permute-start(bf16[2,32,128,128]{3,2,1,0:T(8,128)(2,1)S(1)} %broadcast_select_fusion), channel_id=1, source_target_pairs={{2,0},{3,1},{4,2},{5,3},{6,4},{7,5},{0,6},{1,7},{10,8},{11,9},{12,... | collective-permute-start | bytes 6291464 | tf_op jit(solution)/shard_map/ppermute | solution.py:14
  61.2 53.6 %copy-start.3 = (bf16[4096,64]{0,1:T(8,128)(2,1)S(1)}, bf16[4096,64]{0,1:T(8,128)(2,1)}, u32[]{:S(2)}) copy-start(bf16[4096,64]{0,1:T(8,128)(2,1)} %param.9) | copy-start | bytes 1572868
  107.8 50.5 %collective-permute-start.2 = (bf16[2,32,128,128]{3,2,1,0:T(8,128)(2,1)}, bf16[2,32,128,128]{3,2,1,0:T(8,128)(2,1)S(1)}, u32[]{:S(2)}, u32[]{:S(2)}) collective-permute-start(bf16[2,32,128,128]{3,2,1,0:T(8,128)(2,1)} %broadcast_select_fusion.1), channel_id=1, source_target_pairs={{1,0},{2,1},{3,2},{4,3},{5,4},{6,5},{7,6},{0,7},{9,8},{10,9},{11,1... | collective-permute-start | bytes 6291464 | tf_op jit(solution)/shard_map/ppermute | solution.py:14
  251.5 558.7 %all-reduce.3.cloned.1.call-start = ((), (), s32[]{:S(2)}) async-start(), calls=%async_computation | async-start | bytes 8388608 | tf_op jit(solution)/shard_map/psum | solution.py:130
  590.0 53.4 %copy-start = (f32[128,64,128]{2,0,1:T(8,128)S(1)}, f32[128,64,128]{2,0,1:T(8,128)}, u32[]{:S(2)}) copy-start(f32[128,64,128]{2,0,1:T(8,128)} %get-tuple-element.244) | copy-start | bytes 12582916
  592.7 50.7 %collective-permute-start.3 = (bf16[64,128,128]{2,1,0:T(8,128)(2,1)S(1)}, bf16[64,128,128]{2,1,0:T(8,128)(2,1)S(1)}, u32[]{:S(2)}, u32[]{:S(2)}) collective-permute-start(bf16[64,128,128]{2,1,0:T(8,128)(2,1)S(1)} %bitcast_convert_fusion), channel_id=1, source_target_pairs={{7,0},{0,1},{1,2},{2,3},{3,4},{4,5},{5,6},{6,7},{15,8},{8,9},{9,10... | collective-permute-start | bytes 6291464 | tf_op jit(solution)/shard_map/ppermute | solution.py:14
  644.0 48.9 %collective-permute-start.4 = (bf16[64,128,128]{2,1,0:T(8,128)(2,1)S(1)}, bf16[64,128,128]{2,1,0:T(8,128)(2,1)S(1)}, u32[]{:S(2)}, u32[]{:S(2)}) collective-permute-start(bf16[64,128,128]{2,1,0:T(8,128)(2,1)S(1)} %fusion.10), channel_id=1, source_target_pairs={{6,0},{7,1},{0,2},{1,3},{2,4},{3,5},{4,6},{5,7},{14,8},{15,9},{8,1... | collective-permute-start | bytes 6291464 | tf_op jit(solution)/shard_map/ppermute | solution.py:14
  694.2 2.0 copy-start.1
  696.4 26.5 %collective-permute-start.5 = (bf16[32,128,128]{2,1,0:T(8,128)(2,1)S(1)}, bf16[32,128,128]{2,1,0:T(8,128)(2,1)S(1)}, u32[]{:S(2)}, u32[]{:S(2)}) collective-permute-start(bf16[32,128,128]{2,1,0:T(8,128)(2,1)S(1)} %slice.43), channel_id=1, source_target_pairs={{7,0},{0,1},{1,2},{2,3},{3,4},{4,5},{5,6},{6,7},{15,8},{8,9},{9,10... | collective-permute-start | bytes 3145736 | tf_op jit(solution)/shard_map/ppermute | solution.py:14
  727.4 82.8 %copy-start.2 = (bf16[2,32,128,128]{3,2,1,0:T(8,128)(2,1)S(1)}, bf16[2,32,128,128]{3,2,1,0:T(8,128)(2,1)}, u32[]{:S(2)}) copy-start(bf16[2,32,128,128]{3,2,1,0:T(8,128)(2,1)} %param.8) | copy-start | bytes 6291460
Sparse Core Ops, SparseCore 0:
  251.6 127.8 all-gather.2
  727.5 82.5 all-reduce.2
